TPU v7x, 32 devices: a whole 2x2x4 slice. The times are simulated.
32 devices in a mesh: dp: 8 (over z, x), fsdp: 4 (over y, core).
Axes of the slice: x: 2, y: 2, z: 4, core: 2. Of those that a mesh axis runs over, the one named last changes fastest.
Arguments:
- latents: float32 [96, 256, 384], P(('dp', 'fsdp')), may hold values from -6 to 6
- conditioning: float32 [96, 384], P(('dp', 'fsdp')), may hold values from -6 to 6
- seq_counts: int32 [32], P(('dp', 'fsdp')), may hold values from 1 to 3, as said below
- cotangent: float32 [96, 256, 384], P(('dp', 'fsdp')), may hold values from -6 to 6
- ada_weight: bfloat16 [2, 384, 2304], P(None, 'fsdp'), may hold values from -0.3125 to 0.3125
- ada_bias: bfloat16 [2, 2304], P(None, 'fsdp'), may hold values from -2.390625 to 2.390625
- qkv_weight: bfloat16 [2, 384, 1152], P(None, 'fsdp'), may hold values from -0.3125 to 0.3125
- proj_weight: bfloat16 [2, 384, 384], P(None, 'fsdp'), may hold values from -6 to 6
- proj_bias: bfloat16 [2, 384], P(None, 'fsdp'), may hold values from -3.59375 to 3.59375
- up_weight: bfloat16 [2, 384, 1536], P(None, 'fsdp'), may hold values from -0.3125 to 0.3125
- up_bias: bfloat16 [2, 1536], P(None, 'fsdp'), may hold values from -3.59375 to 3.59375
- down_weight: bfloat16 [2, 1536, 384], P(None, 'fsdp'), may hold values from -0.15625 to 0.15625
- down_bias: bfloat16 [2, 384], P(None, 'fsdp'), may hold values from -3.59375 to 3.59375
Outputs:
- block_out: float32 [96, 256, 384], P(('dp', 'fsdp'))
- grad_latents: float32 [96, 256, 384], P(('dp', 'fsdp'))
- grad_conditioning: float32 [96, 384], P(('dp', 'fsdp'))
- grad_ada_weight: float32 [2, 384, 2304], P(None, 'fsdp')
- grad_ada_bias: float32 [2, 2304], P(None, 'fsdp')
- grad_qkv_weight: float32 [2, 384, 1152], P(None, 'fsdp')
- grad_proj_weight: float32 [2, 384, 384], P(None, 'fsdp')
- grad_proj_bias: float32 [2, 384], P(None, 'fsdp')
- grad_up_weight: float32 [2, 384, 1536], P(None, 'fsdp')
- grad_up_bias: float32 [2, 1536], P(None, 'fsdp')
- grad_down_weight: float32 [2, 1536, 384], P(None, 'fsdp')
- grad_down_bias: float32 [2, 384], P(None, 'fsdp')
Inputs may be any that keep to these rules, and one draw needn't show every extreme that they name: `seq_counts`: number of live sequences of a device; its slots from that number on are padding.
All inputs are finite; a program needn't handle non-finite values.
Results may differ from a plain program's by a relative error of at most 0.014.
Values may be sent and summed in bfloat16 or wider, within the bound.
No kernel may reach another device: no remote copies, remote signals or barrier semaphores. Data moves between devices by JAX's collectives and lax.ppermute only.
A program may use at most 192 MiB of HBM per device.

v0:
```python
import jax
import jax.numpy as jnp
from jax import lax
from jax.sharding import PartitionSpec as P

HEADS = 6
LAYERS = 2
NORM_EPS = 1e-06
GELU_K = 0.7978845608028654
GELU_C = 0.044715


def einsum_mixed(form, left, right):
    return jnp.einsum(form, left, right, preferred_element_type=jnp.float32)


def matmul_last(left, right):
    flat = left.reshape(-1, left.shape[-1])
    return jnp.dot(flat, right, preferred_element_type=jnp.float32).reshape(
        left.shape[:-1] + (right.shape[1],)
    )


def matmul_back(left, right):
    flat = left.reshape(-1, left.shape[-1])
    return jnp.dot(flat, right.T, preferred_element_type=jnp.float32).reshape(
        left.shape[:-1] + (right.shape[0],)
    )


def outer_total(left, right):
    return jnp.dot(
        left.reshape(-1, left.shape[-1]).T,
        right.reshape(-1, right.shape[-1]),
        preferred_element_type=jnp.float32,
    )


def norm_rows(values):
    center = values - jnp.mean(values, axis=-1, keepdims=True)
    inv_std = lax.rsqrt(jnp.mean(center * center, axis=-1, keepdims=True) + NORM_EPS)
    return (center * inv_std, inv_std)


def norm_back(normed, inv_std, grad_normed):
    mean_grad = jnp.mean(grad_normed, axis=-1, keepdims=True)
    mean_prod = jnp.mean(grad_normed * normed, axis=-1, keepdims=True)
    return inv_std * (grad_normed - mean_grad - normed * mean_prod)


def gelu_tanh(values):
    inner = GELU_K * (values + GELU_C * values * values * values)
    return 0.5 * values * (1.0 + jnp.tanh(inner))


def gelu_slope(values):
    tangent = jnp.tanh(GELU_K * (values + GELU_C * values * values * values))
    return 0.5 * (1.0 + tangent) + 0.5 * values * (1.0 - tangent * tangent) * GELU_K * (
        1.0 + 3.0 * GELU_C * values * values
    )


def silu_slope(values):
    sigm = jax.nn.sigmoid(values)
    return sigm * (1.0 + values * (1.0 - sigm))


def split_heads(qkv):
    seq_slots, length, triple = qkv.shape
    width = triple // 3
    split = qkv.reshape(seq_slots, length, 3, HEADS, width // HEADS)
    return (split[:, :, 0], split[:, :, 1], split[:, :, 2])


def attend(qkv):
    queries, keys, values = split_heads(qkv)
    scale = 1.0 / jnp.sqrt(jnp.float32(queries.shape[-1]))
    scores = einsum_mixed("sqhd,skhd->shqk", queries, keys) * scale
    top = jnp.max(scores, axis=-1, keepdims=True)
    expo = jnp.exp(scores - top)
    probs = expo / jnp.sum(expo, axis=-1, keepdims=True)
    probs_low = probs.astype(jnp.bfloat16)
    mixed = einsum_mixed("shqk,skhd->sqhd", probs_low, values).astype(jnp.bfloat16)
    return (probs, probs_low, mixed.reshape(qkv.shape[0], qkv.shape[1], -1))


def attend_back(qkv, probs, probs_low, grad_mixed):
    queries, keys, values = split_heads(qkv)
    scale = 1.0 / jnp.sqrt(jnp.float32(queries.shape[-1]))
    grad_heads = grad_mixed.reshape(values.shape)
    grad_probs = einsum_mixed("sqhd,skhd->shqk", grad_heads, values)
    grad_values = einsum_mixed("shqk,sqhd->skhd", probs_low, grad_heads)
    row_dot = jnp.sum(probs * grad_probs, axis=-1, keepdims=True)
    grad_scores = (probs * (grad_probs - row_dot) * scale).astype(jnp.bfloat16)
    grad_queries = einsum_mixed("shqk,skhd->sqhd", grad_scores, keys)
    grad_keys = einsum_mixed("shqk,sqhd->skhd", grad_scores, queries)
    joined = jnp.stack([grad_queries, grad_keys, grad_values], axis=2)
    return joined.reshape(qkv.shape).astype(jnp.bfloat16)


def layer_parts(resid, cond, weights):
    (
        ada_weight,
        ada_bias,
        qkv_weight,
        proj_weight,
        proj_bias,
        up_weight,
        up_bias,
        down_weight,
        down_bias,
    ) = weights
    width = resid.shape[-1]
    act_low = jax.nn.silu(cond).astype(jnp.bfloat16)
    ada = jnp.dot(act_low, ada_weight, preferred_element_type=jnp.float32) + ada_bias.astype(
        jnp.float32
    )
    mods = [ada[:, None, piece_idx * width : (piece_idx + 1) * width] for piece_idx in range(6)]
    normed_one, inv_one = norm_rows(resid)
    attn_in = (normed_one * (1.0 + mods[1]) + mods[0]).astype(jnp.bfloat16)
    qkv = matmul_last(attn_in, qkv_weight).astype(jnp.bfloat16)
    probs, probs_low, mixed = attend(qkv)
    attn = matmul_last(mixed, proj_weight) + proj_bias.astype(jnp.float32)
    resid_one = resid + mods[2] * attn
    normed_two, inv_two = norm_rows(resid_one)
    mlp_in = (normed_two * (1.0 + mods[4]) + mods[3]).astype(jnp.bfloat16)
    pre_act = matmul_last(mlp_in, up_weight) + up_bias.astype(jnp.float32)
    hidden = gelu_tanh(pre_act).astype(jnp.bfloat16)
    branch = matmul_last(hidden, down_weight) + down_bias.astype(jnp.float32)
    result = resid_one + mods[5] * branch
    return dict(
        act_low=act_low,
        mods=mods,
        normed_one=normed_one,
        inv_one=inv_one,
        attn_in=attn_in,
        qkv=qkv,
        probs=probs,
        probs_low=probs_low,
        mixed=mixed,
        attn=attn,
        normed_two=normed_two,
        inv_two=inv_two,
        mlp_in=mlp_in,
        pre_act=pre_act,
        hidden=hidden,
        branch=branch,
        result=result,
    )


def layer_backward(resid, cond, weights, grad_out):
    (
        ada_weight,
        ada_bias,
        qkv_weight,
        proj_weight,
        proj_bias,
        up_weight,
        up_bias,
        down_weight,
        down_bias,
    ) = weights
    saved = layer_parts(resid, cond, weights)
    mods = saved["mods"]
    grad_gate_two = jnp.sum(grad_out * saved["branch"], axis=1)
    grad_branch = grad_out * mods[5]
    grad_down_bias = jnp.sum(grad_branch, axis=(0, 1))
    branch_low = grad_branch.astype(jnp.bfloat16)
    grad_down_weight = outer_total(saved["hidden"], branch_low)
    grad_pre = matmul_back(branch_low, down_weight) * gelu_slope(saved["pre_act"])
    grad_up_bias = jnp.sum(grad_pre, axis=(0, 1))
    pre_low = grad_pre.astype(jnp.bfloat16)
    grad_up_weight = outer_total(saved["mlp_in"], pre_low)
    grad_mlp = matmul_back(pre_low, up_weight)
    grad_shift_two = jnp.sum(grad_mlp, axis=1)
    grad_scale_two = jnp.sum(grad_mlp * saved["normed_two"], axis=1)
    grad_one = grad_out + norm_back(
        saved["normed_two"], saved["inv_two"], grad_mlp * (1.0 + mods[4])
    )
    grad_gate_one = jnp.sum(grad_one * saved["attn"], axis=1)
    grad_attn = grad_one * mods[2]
    grad_proj_bias = jnp.sum(grad_attn, axis=(0, 1))
    attn_low = grad_attn.astype(jnp.bfloat16)
    grad_proj_weight = outer_total(saved["mixed"], attn_low)
    grad_mixed = matmul_back(attn_low, proj_weight).astype(jnp.bfloat16)
    grad_qkv = attend_back(saved["qkv"], saved["probs"], saved["probs_low"], grad_mixed)
    grad_qkv_weight = outer_total(saved["attn_in"], grad_qkv)
    grad_in = matmul_back(grad_qkv, qkv_weight)
    grad_shift_one = jnp.sum(grad_in, axis=1)
    grad_scale_one = jnp.sum(grad_in * saved["normed_one"], axis=1)
    grad_resid = grad_one + norm_back(
        saved["normed_one"], saved["inv_one"], grad_in * (1.0 + mods[1])
    )
    grad_ada = jnp.concatenate(
        [
            grad_shift_one,
            grad_scale_one,
            grad_gate_one,
            grad_shift_two,
            grad_scale_two,
            grad_gate_two,
        ],
        axis=-1,
    )
    grad_ada_bias = jnp.sum(grad_ada, axis=0)
    ada_low = grad_ada.astype(jnp.bfloat16)
    grad_ada_weight = jnp.dot(saved["act_low"].T, ada_low, preferred_element_type=jnp.float32)
    grad_cond = jnp.dot(ada_low, ada_weight.T, preferred_element_type=jnp.float32) * silu_slope(
        cond
    )
    grads = (
        grad_ada_weight,
        grad_ada_bias,
        grad_qkv_weight,
        grad_proj_weight,
        grad_proj_bias,
        grad_up_weight,
        grad_up_bias,
        grad_down_weight,
        grad_down_bias,
    )
    return (grad_resid, grad_cond, grads)


def gather_forward(stacks, layer_idx):
    (
        ada_weight,
        ada_bias,
        qkv_weight,
        proj_weight,
        proj_bias,
        up_weight,
        up_bias,
        down_weight,
        down_bias,
    ) = stacks
    return (
        lax.all_gather(ada_weight[layer_idx], "fsdp", axis=0, tiled=True),
        lax.all_gather(ada_bias[layer_idx], "fsdp", axis=0, tiled=True),
        lax.all_gather(qkv_weight[layer_idx], "fsdp", axis=0, tiled=True),
        lax.all_gather(proj_weight[layer_idx], "fsdp", axis=0, tiled=True),
        lax.all_gather(proj_bias[layer_idx], "fsdp", axis=0, tiled=True),
        lax.all_gather(up_weight[layer_idx], "fsdp", axis=0, tiled=True),
        lax.all_gather(up_bias[layer_idx], "fsdp", axis=0, tiled=True),
        lax.all_gather(down_weight[layer_idx], "fsdp", axis=0, tiled=True),
        lax.all_gather(down_bias[layer_idx], "fsdp", axis=0, tiled=True),
    )


def gather_backward(stacks, layer_idx):
    (
        ada_weight,
        ada_bias,
        qkv_weight,
        proj_weight,
        proj_bias,
        up_weight,
        up_bias,
        down_weight,
        down_bias,
    ) = stacks
    return (
        lax.all_gather(ada_weight[layer_idx], "fsdp", axis=0, tiled=True),
        lax.all_gather(ada_bias[layer_idx], "fsdp", axis=0, tiled=True),
        lax.all_gather(qkv_weight[layer_idx], "fsdp", axis=0, tiled=True),
        lax.all_gather(proj_weight[layer_idx], "fsdp", axis=0, tiled=True),
        lax.all_gather(proj_bias[layer_idx], "fsdp", axis=0, tiled=True),
        lax.all_gather(up_weight[layer_idx], "fsdp", axis=0, tiled=True),
        lax.all_gather(up_bias[layer_idx], "fsdp", axis=0, tiled=True),
        lax.all_gather(down_weight[layer_idx], "fsdp", axis=0, tiled=True),
        lax.all_gather(down_bias[layer_idx], "fsdp", axis=0, tiled=True),
    )


def reduce_layer(grads):
    shards = (
        lax.psum_scatter(grads[0], "fsdp", scatter_dimension=0, tiled=True),
        lax.psum_scatter(grads[1], "fsdp", scatter_dimension=0, tiled=True),
        lax.psum_scatter(grads[2], "fsdp", scatter_dimension=0, tiled=True),
        lax.psum_scatter(grads[3], "fsdp", scatter_dimension=0, tiled=True),
        lax.psum_scatter(grads[4], "fsdp", scatter_dimension=0, tiled=True),
        lax.psum_scatter(grads[5], "fsdp", scatter_dimension=0, tiled=True),
        lax.psum_scatter(grads[6], "fsdp", scatter_dimension=0, tiled=True),
        lax.psum_scatter(grads[7], "fsdp", scatter_dimension=0, tiled=True),
        lax.psum_scatter(grads[8], "fsdp", scatter_dimension=0, tiled=True),
    )
    return lax.psum(
        (
            shards[0],
            shards[1],
            shards[2],
            shards[3],
            shards[4],
            shards[5],
            shards[6],
            shards[7],
            shards[8],
        ),
        "dp",
    )


def on_device(
    latents,
    conditioning,
    seq_counts,
    cotangent,
    ada_weight,
    ada_bias,
    qkv_weight,
    proj_weight,
    proj_bias,
    up_weight,
    up_bias,
    down_weight,
    down_bias,
):
    stacks = (
        ada_weight,
        ada_bias,
        qkv_weight,
        proj_weight,
        proj_bias,
        up_weight,
        up_bias,
        down_weight,
        down_bias,
    )
    seq_slots = latents.shape[0]
    live = (jnp.arange(seq_slots, dtype=jnp.int32) < seq_counts[0]).astype(jnp.float32)[
        :, None, None
    ]
    inputs = []
    gathered = []
    current = latents
    for layer_idx in range(LAYERS):
        weights = gather_forward(stacks, layer_idx)
        gathered.append(weights)
        inputs.append(current)
        current = layer_parts(current, conditioning, weights)["result"]
    block_out = current * live
    grad = cotangent * live
    grad_cond = jnp.zeros(conditioning.shape, jnp.float32)
    layer_grads = [None] * LAYERS
    for layer_idx in reversed(range(LAYERS)):
        weights = gather_backward(stacks, layer_idx)
        grad, cond_part, grads = layer_backward(inputs[layer_idx], conditioning, weights, grad)
        grad_cond = grad_cond + cond_part
        layer_grads[layer_idx] = reduce_layer(grads)
    finals = [
        jnp.stack([layer_grads[layer_idx][piece_idx] for layer_idx in range(LAYERS)], axis=0)
        for piece_idx in range(9)
    ]
    return (
        block_out,
        grad,
        grad_cond,
        finals[0],
        finals[1],
        finals[2],
        finals[3],
        finals[4],
        finals[5],
        finals[6],
        finals[7],
        finals[8],
    )


def solution(mesh):
    in_specs = (
        P(("dp", "fsdp"), None, None),
        P(("dp", "fsdp"), None),
        P(("dp", "fsdp")),
        P(("dp", "fsdp"), None, None),
        P(None, "fsdp", None),
        P(None, "fsdp"),
        P(None, "fsdp", None),
        P(None, "fsdp", None),
        P(None, "fsdp"),
        P(None, "fsdp", None),
        P(None, "fsdp"),
        P(None, "fsdp", None),
        P(None, "fsdp"),
    )
    out_specs = (
        P(("dp", "fsdp"), None, None),
        P(("dp", "fsdp"), None, None),
        P(("dp", "fsdp"), None),
        P(None, "fsdp", None),
        P(None, "fsdp"),
        P(None, "fsdp", None),
        P(None, "fsdp", None),
        P(None, "fsdp"),
        P(None, "fsdp", None),
        P(None, "fsdp"),
        P(None, "fsdp", None),
        P(None, "fsdp"),
    )
    return jax.shard_map(
        on_device, mesh=mesh, in_specs=in_specs, out_specs=out_specs, check_vma=False
    )
```

profile of v0, /device:TPU:0, one launch (start us, length us, event | category | flops | bytes accessed | tf_op | source)
XLA Modules:
  0.0 733.3 jit_solution(9864900961176631379)
XLA Ops:
  17.1 6.2 all-gather.15
  31.0 11.7 %all-reduce.17 = (bf16[2304]{0:T(1024)(128)(2,1)S(1)}, bf16[384]{0:T(512)(128)(2,1)S(1)}, bf16[384]{0:T(512)(128)(2,1)S(1)}, bf16[2304]{0:T(1024)(128)(2,1)S(1)}...) all-reduce(bf16[2304]{0:T(1024)(128)(2,1)S(1)} %dynamic-update-slice, ...), channel_id=3, replica_groups=mesh['dp'=8,'fsdp'=4] {'fsdp'}, use_global_device_ids=true, to_apply=%add | all-reduce | flops 6144 | bytes 24576
  43.9 8.0 %all-gather.12 = bf16[1,384,384]{2,1,0:T(8,128)(2,1)} all-gather(bf16[1,96,384]{2,1,0:T(8,128)(2,1)S(1)} %get-tuple-element.91), channel_id=14, replica_groups=mesh['dp'=8,'fsdp'=4] {'fsdp'}, dimensions={1}, use_global_device_ids=true | all-gather | bytes 368640 | tf_op jit(solution)/shard_map/all_gather | solution.py:242
  51.9 7.2 all-gather.3
  59.1 9.7 %all-gather.11 = bf16[1,384,1152]{2,1,0:T(8,128)(2,1)} all-gather(bf16[1,96,1152]{2,1,0:T(8,128)(2,1)S(1)} %get-tuple-element.89), channel_id=13, replica_groups=mesh['dp'=8,'fsdp'=4] {'fsdp'}, dimensions={1}, use_global_device_ids=true | all-gather | bytes 1105920 | tf_op jit(solution)/shard_map/all_gather | solution.py:241
  68.8 13.9 %all-gather.2 = bf16[1,384,1152]{2,1,0:T(8,128)(2,1)S(1)} all-gather(bf16[1,96,1152]{2,1,0:T(8,128)(2,1)S(1)} %get-tuple-element.90), channel_id=4, replica_groups=mesh['dp'=8,'fsdp'=4] {'fsdp'}, dimensions={1}, use_global_device_ids=true | all-gather | bytes 1105920 | tf_op jit(solution)/shard_map/all_gather | solution.py:241
  106.1 5.7 fusion.135
  141.0 7.6 %fusion.148 = (f32[1536]{0:T(1024)}, bf16[3,256,1536]{2,1,0:T(8,128)(2,1)S(1)}) fusion(f32[3,256,1536]{2,1,0:T(8,128)} %fusion.82, f32[1536]{0:T(1024)} %convert_reduce_fusion, bf16[1,1536,384]{2,1,0:T(8,128)(2,1)} %all-gather.35.cloned.1.call-done, f32[3,256,384]{2,1,0:T(8,128)} %param.16, f32[3]{0:T(128)} %compare_convert_fusion, ...), kind=kOutput, calls=%fused_computation.256 | convolution fusion | flops 931625472 | bytes 9454092 | tf_op jit(solution)/shard_map/dot_general | solution.py:26
  170.8 9.1 %fusion.67 = bf16[3,256,1,6,64]{1,4,3,0,2:T(8,128)(2,1)} fusion(f32[3,6,256,256]{2,3,1,0:T(8,128)} %fusion.112, bf16[3,256,3,6,64]{1,4,3,2,0:T(8,128)(2,1)} %bitcast.237, f32[3,6,256,256]{2,3,1,0:T(8,128)} %copy-done.18, f32[3,6,256]{2,1,0:T(8,128)} %copy-done.81), kind=kOutput, calls=%fused_computation.80 | convolution fusion | flops 159552256 | bytes 20103168 | tf_op jit(solution)/shard_map/shqk,skhd->sqhd/dot_general | solution.py:14
  179.8 8.9 %fusion.64 = bf16[3,256,1,6,64]{1,4,3,0,2:T(8,128)(2,1)} fusion(f32[3,6,256,256]{2,3,1,0:T(8,128)} %fusion.112, bf16[3,256,3,6,64]{1,4,3,2,0:T(8,128)(2,1)} %bitcast.238, f32[3,6,256,256]{2,3,1,0:T(8,128)} %copy-done.18, f32[3,6,256]{2,1,0:T(8,128)} %copy-done.81), kind=kOutput, calls=%fused_computation.79 | convolution fusion | flops 159552256 | bytes 20103168 | tf_op jit(solution)/shard_map/shqk,sqhd->skhd/dot_general | solution.py:14
  225.4 9.0 %fusion.73 = bf16[3,256,1,6,64]{1,4,3,0,2:T(8,128)(2,1)} fusion(f32[3,6,256,256]{2,3,1,0:T(8,128)} %fusion.110, bf16[3,256,3,6,64]{1,4,3,2,0:T(8,128)(2,1)} %bitcast.232, f32[3,6,256,256]{2,3,1,0:T(8,128)} %copy-done.17, f32[3,6,256]{2,1,0:T(8,128)} %copy-done.80), kind=kOutput, calls=%fused_computation.82 | convolution fusion | flops 159552256 | bytes 20103168 | tf_op jit(solution)/shard_map/shqk,skhd->sqhd/dot_general | solution.py:14
  234.4 9.0 %fusion.70 = bf16[3,256,1,6,64]{1,4,3,0,2:T(8,128)(2,1)} fusion(f32[3,6,256,256]{2,3,1,0:T(8,128)} %fusion.110, bf16[3,256,3,6,64]{1,4,3,2,0:T(8,128)(2,1)} %bitcast.233, f32[3,6,256,256]{2,3,1,0:T(8,128)} %copy-done.17, f32[3,6,256]{2,1,0:T(8,128)} %copy-done.80), kind=kOutput, calls=%fused_computation.81 | convolution fusion | flops 159552256 | bytes 20103168 | tf_op jit(solution)/shard_map/shqk,sqhd->skhd/dot_general | solution.py:14
  251.1 6.5 convolution_bitcast_fusion
  263.3 6.3 convolution_bitcast_fusion.1
  286.0 16.1 %reduce-scatter.15.cloned.1.call-done = f32[96,1152]{1,0:T(8,128)} async-done(((f32[384,1152]{1,0:T(8,128)}), f32[96,1152]{1,0:T(8,128)}) %reduce-scatter.15.cloned.1.call-update) | async-done | bytes 442384 | tf_op jit(solution)/shard_map/reduce_scatter | solution.py:280
  302.0 35.4 %reduce-scatter.29.cloned.1.call-done = f32[384,384]{1,0:T(8,128)} async-done(((f32[1536,384]{1,0:T(8,128)}), f32[384,384]{1,0:T(8,128)}) %reduce-scatter.29.cloned.1.call-update) | async-done | bytes 589840 | tf_op jit(solution)/shard_map/reduce_scatter | solution.py:285
  337.4 35.2 %reduce-scatter.25.cloned.1.call-done = f32[96,1536]{1,0:T(8,128)} async-done(((f32[384,1536]{1,0:T(8,128)}), f32[96,1536]{1,0:T(8,128)}) %reduce-scatter.25.cloned.1.call-update) | async-done | bytes 589840 | tf_op jit(solution)/shard_map/reduce_scatter | solution.py:283
  372.6 35.4 %reduce-scatter.27.cloned.1.call-done = f32[384,384]{1,0:T(8,128)} async-done(((f32[1536,384]{1,0:T(8,128)}), f32[384,384]{1,0:T(8,128)}) %reduce-scatter.27.cloned.1.call-update) | async-done | bytes 589840 | tf_op jit(solution)/shard_map/reduce_scatter | solution.py:285
  408.0 35.2 %reduce-scatter.23.cloned.1.call-done = f32[96,1536]{1,0:T(8,128)} async-done(((f32[384,1536]{1,0:T(8,128)}), f32[96,1536]{1,0:T(8,128)}) %reduce-scatter.23.cloned.1.call-update) | async-done | bytes 589840 | tf_op jit(solution)/shard_map/reduce_scatter | solution.py:283
  443.3 42.8 %reduce-scatter.13.cloned.1.call-done = f32[96,2304]{1,0:T(8,128)} async-done(((f32[384,2304]{1,0:T(8,128)}), f32[96,2304]{1,0:T(8,128)}) %reduce-scatter.13.cloned.1.call-update) | async-done | bytes 884752 | tf_op jit(solution)/shard_map/reduce_scatter | solution.py:278
  486.1 42.8 %reduce-scatter.11.cloned.1.call-done = f32[96,2304]{1,0:T(8,128)} async-done(((f32[384,2304]{1,0:T(8,128)}), f32[96,2304]{1,0:T(8,128)}) %reduce-scatter.11.cloned.1.call-update) | async-done | bytes 884752 | tf_op jit(solution)/shard_map/reduce_scatter | solution.py:278
  531.2 10.6 %all-reduce.16 = (f32[2304]{0:T(1024)S(1)}, f32[2304]{0:T(1024)S(1)}, f32[384]{0:T(512)S(1)}, f32[384]{0:T(512)S(1)}, f32[1536]{0:T(1024)S(1)}, /*index=5*/f32[1536]{0:T(1024)S(1)}, f32[384]{0:T(512)S(1)}, f32[384]{0:T(512)S(1)}) all-reduce(f32[2304]{0:T(1024)S(1)} %reduce_sum.433, ...), channel_id=23, replica_groups=mesh['dp'=8,'fsdp'=4] {'fsdp'}, use_global_device_ids=true, to_apply=%region_42.43.clone | all-reduce | flops 9216 | bytes 73728
  542.4 39.5 %all-reduce.14 = (f32[1,576]{1,0:T(1,128)S(1)}, f32[1,576]{1,0:T(1,128)S(1)}, f32[1,96]{1,0:T(1,128)S(1)}, f32[1,96]{1,0:T(1,128)S(1)}, f32[1,384]{1,0:T(1,128)S...) all-reduce(f32[1,576]{1,0:T(1,128)S(1)} %stack.125, ...), channel_id=1, replica_groups=mesh['dp'=8,'fsdp'=4] {'dp'}, use_global_device_ids=true, to_apply=%region_43.44 | all-reduce | flops 2304 | bytes 18432 | tf_op jit(solution)/shard_map/psum | solution.py:288
  590.4 129.4 %all-reduce.20.cloned.1.call-done = (f32[1,96,2304]{2,1,0:T(8,128)}, f32[1,96,2304]{2,1,0:T(8,128)}, f32[1,96,1152]{2,1,0:T(8,128)}, f32[1,96,1152]{2,1,0:T(8,12...) async-done(((f32[1,96,2304]{2,1,0:T(8,128)}, ...) | async-done | bytes 5308432 | tf_op jit(solution)/shard_map/psum | solution.py:288
  (428 shorter events, 172.7 us)
Async XLA Ops:
  7.2 75.5 %all-gather.25.cloned.1.call-start = ((), (), s32[]{:S(2)}) async-start(), calls=%async_computation.20 | async-start | bytes 2211840 | tf_op jit(solution)/shard_map/all_gather | solution.py:239
  9.5 75.5 %all-gather.31.cloned.1.call-start = ((), (), s32[]{:S(2)}) async-start(), calls=%async_computation.23 | async-start | bytes 2211840 | tf_op jit(solution)/shard_map/all_gather | solution.py:239
  10.3 91.0 %all-gather.27.cloned.1.call-start = ((), (), s32[]{:S(2)}) async-start(), calls=%async_computation.21 | async-start | bytes 1474560 | tf_op jit(solution)/shard_map/all_gather | solution.py:244
  11.2 94.9 %all-gather.29.cloned.1.call-start = ((), (), s32[]{:S(2)}) async-start(), calls=%async_computation.22 | async-start | bytes 1474560 | tf_op jit(solution)/shard_map/all_gather | solution.py:246
  12.1 31.7 %copy-start.52 = (bf16[2,96,384]{2,1,0:T(8,128)(2,1)S(1)}, bf16[2,96,384]{2,1,0:T(8,128)(2,1)}, u32[]{:S(2)}) copy-start(bf16[2,96,384]{2,1,0:T(8,128)(2,1)} %param.20) | copy-start | bytes 442372
  12.2 119.2 %all-gather.33.cloned.1.call-start = ((), (), s32[]{:S(2)}) async-start(), calls=%async_computation.24 | async-start | bytes 1474560 | tf_op jit(solution)/shard_map/all_gather | solution.py:244
  12.8 128.2 %all-gather.35.cloned.1.call-start = ((), (), s32[]{:S(2)}) async-start(), calls=%async_computation.25 | async-start | bytes 1474560 | tf_op jit(solution)/shard_map/all_gather | solution.py:246
  13.3 272.6 %reduce-scatter.21.cloned.1.call-start = ((), (), s32[]{:S(2)}) async-start(), calls=%async_computation.15 | async-start | bytes 737280 | tf_op jit(solution)/shard_map/reduce_scatter | solution.py:281
  16.5 42.6 %copy-start.48 = (bf16[2,96,1152]{2,1,0:T(8,128)(2,1)S(1)}, bf16[2,96,1152]{2,1,0:T(8,128)(2,1)}, u32[]{:S(2)}) copy-start(bf16[2,96,1152]{2,1,0:T(8,128)(2,1)} %param.19) | copy-start | bytes 1327108
  16.7 70.7 %copy-start.66 = (f32[3,256]{1,0:T(4,128)}, f32[3,256]{1,0:T(4,128)S(1)}, u32[]{:S(2)}) copy-start(f32[3,256]{1,0:T(4,128)S(1)} %broadcast_multiply_fusion.11) | copy-start | bytes 9220
  17.1 70.4 %copy-start.82 = (f32[3,256]{1,0:T(4,128)}, f32[3,256]{1,0:T(4,128)S(1)}, u32[]{:S(2)}) copy-start(f32[3,256]{1,0:T(4,128)S(1)} %add_rsqrt_fusion.3) | copy-start | bytes 9220
  29.6 76.5 %copy-start.91 = (f32[1536]{0:T(1024)}, f32[1536]{0:T(1024)S(1)}, u32[]{:S(2)}) copy-start(f32[1536]{0:T(1024)S(1)} %convert_reduce_fusion.1) | copy-start | bytes 18436
  59.1 40.1 %copy-start.19 = (bf16[1,384,384]{2,1,0:T(8,128)(2,1)}, bf16[1,384,384]{2,1,0:T(8,128)(2,1)S(1)}, u32[]{:S(2)}) copy-start(bf16[1,384,384]{2,1,0:T(8,128)(2,1)S(1)} %all-gather.3) | copy-start | bytes 884740
  191.9 94.1 %reduce-scatter.19.cloned.1.call-start = ((), (), s32[]{:S(2)}) async-start(), calls=%async_computation.14 | async-start | bytes 737280 | tf_op jit(solution)/shard_map/reduce_scatter | solution.py:281
  211.9 74.0 %reduce-scatter.17.cloned.1.call-start = ((), (), s32[]{:S(2)}) async-start(), calls=%async_computation.13 | async-start | bytes 2211840 | tf_op jit(solution)/shard_map/reduce_scatter | solution.py:280
  216.4 85.7 %reduce-scatter.15.cloned.1.call-start = ((), (), s32[]{:S(2)}) async-start(), calls=%async_computation.12 | async-start | bytes 2211840 | tf_op jit(solution)/shard_map/reduce_scatter | solution.py:280
  251.1 86.3 %reduce-scatter.29.cloned.1.call-start = ((), (), s32[]{:S(2)}) async-start(), calls=%async_computation.19 | async-start | bytes 2949120 | tf_op jit(solution)/shard_map/reduce_scatter | solution.py:285
  257.6 115.0 %reduce-scatter.25.cloned.1.call-start = ((), (), s32[]{:S(2)}) async-start(), calls=%async_computation.17 | async-start | bytes 2949120 | tf_op jit(solution)/shard_map/reduce_scatter | solution.py:283
  262.1 145.9 %reduce-scatter.27.cloned.1.call-start = ((), (), s32[]{:S(2)}) async-start(), calls=%async_computation.18 | async-start | bytes 2949120 | tf_op jit(solution)/shard_map/reduce_scatter | solution.py:285
  269.7 173.6 %reduce-scatter.23.cloned.1.call-start = ((), (), s32[]{:S(2)}) async-start(), calls=%async_computation.16 | async-start | bytes 2949120 | tf_op jit(solution)/shard_map/reduce_scatter | solution.py:283
  274.8 211.3 %reduce-scatter.13.cloned.1.call-start = ((), (), s32[]{:S(2)}) async-start(), calls=%async_computation.11 | async-start | bytes 4423680 | tf_op jit(solution)/shard_map/reduce_scatter | solution.py:278
  278.0 250.9 %reduce-scatter.11.cloned.1.call-start = ((), (), s32[]{:S(2)}) async-start(), calls=%async_computation.10 | async-start | bytes 4423680 | tf_op jit(solution)/shard_map/reduce_scatter | solution.py:278
  285.9 434.0 %all-reduce.20.cloned.1.call-start = ((), (), s32[]{:S(2)}) async-start(), calls=%async_computation.26 | async-start | bytes 10616832 | tf_op jit(solution)/shard_map/psum | solution.py:288
  529.0 57.4 %copy-start.7 = (bf16[1,384,2304]{2,1,0:T(8,128)(2,1)S(1)}, bf16[1,384,2304]{2,1,0:T(8,128)(2,1)}, u32[]{:S(2)}) copy-start(bf16[1,384,2304]{2,1,0:T(8,128)(2,1)} %all-gather.25.cloned.1.call-done) | copy-start | bytes 5308420
  (114 other events, 473.7 us)
Sparse Core Ops, SparseCore 0:
  10.1 23.4 all-gather.24
  35.8 23.4 all-gather.30
  61.5 21.6 all-gather.26
  85.1 17.4 all-gather.28
  104.0 17.4 all-gather.32
  123.5 17.4 all-gather.34
  192.0 22.0 reduce-scatter.20
  216.5 22.0 reduce-scatter.18
  241.2 29.1 reduce-scatter.16
  272.8 29.1 reduce-scatter.14
  304.6 32.7 reduce-scatter.28
  339.8 32.8 reduce-scatter.24
  375.2 32.8 reduce-scatter.26
  410.4 32.8 reduce-scatter.22
  445.7 40.3 reduce-scatter.12
  488.5 40.3 reduce-scatter.10
  533.5 186.2 all-reduce.19
where the time goes:
time: 738 us; the launch traced here: 733 us
  waiting for transfers between devices  379 us (51%)
  matrix products  156 us (21%)
  blocking collectives  112 us (15%)
  local copies, waits for them, and re-layouts  36.4 us (5%)
  other arithmetic  29 us (4%)
  between operations  19.4 us (3%)
    psum x1, waiting for transfers between devices, reduce_layer(): lax.psum((shards[0], shards[1], shards[2], shards[3], shards[4], shards[5...  129 us
    reduce_scatter x2, waiting for transfers between devices, reduce_layer(): lax.psum_scatter(grads[0], 'fsdp', scatter_dimension=0, tiled=True)  85.7 us
    reduce_scatter x2, waiting for transfers between devices, reduce_layer(): lax.psum_scatter(grads[7], 'fsdp', scatter_dimension=0, tiled=True)  70.7 us
    reduce_scatter x2, waiting for transfers between devices, reduce_layer(): lax.psum_scatter(grads[5], 'fsdp', scatter_dimension=0, tiled=True)  70.5 us
    dot_general x12, matrix products, einsum_mixed(): return jnp.einsum(form, left, right, preferred_element_type=jnp.float32)  57.6 us
    psum x1, blocking collectives, reduce_layer(): lax.psum((shards[0], shards[1], shards[2], shards[3], shards[4], shards[5...  39.5 us
    dot_general x8, matrix products, outer_total(): jnp.dot(left.reshape(-1, left.shape[-1]).T, right.reshape(-1, right.shape...  31.1 us
    dot_general x8, matrix products, matmul_last(): jnp.dot(flat, right, preferred_element_type=jnp.float32)  28.3 us
  transfers between devices with their start and end apart: 17, of which 9 were waited for; matrix products, arithmetic and copies ran while one was open for 20% of the time, Pallas kernels for 0%

commit v1 on v0

--- a/solution.py
+++ b/solution.py
@@ -8,6 +8,33 @@
 NORM_EPS = 1e-06
 GELU_K = 0.7978845608028654
 GELU_C = 0.044715
+
+
+def arrange_regions(my_data):
+    far_arr = lax.axis_size("fsdp")
+    near = lax.axis_index("fsdp")
+    small, b_next, reply = (far_arr, near, my_data.shape[0])
+    arr_out = range(small)
+    b_now = map(lambda q: (q, (q + 1) % small), arr_out)
+    history = list(b_now)
+    outcome_arr = range(small)
+    out_arr = map(lambda q: (q, (q - 1) % small), outcome_arr)
+    after = jnp.zeros((*my_data.shape[:0], small * reply, *my_data.shape[1:]), my_data.dtype)
+    after = lax.dynamic_update_slice_in_dim(after, my_data, b_next * reply, axis=0)
+    v_next = oldest = my_data
+    back = small // 2
+    in_order = list(out_arr)
+    for dev_j in range(1, back + 1):
+        v_next = lax.ppermute(v_next, "fsdp", history)
+        after = lax.dynamic_update_slice_in_dim(
+            after, v_next, (b_next - dev_j) % small * reply, axis=0
+        )
+        if dev_j < small - back:
+            oldest = lax.ppermute(oldest, perm=in_order, axis_name="fsdp")
+            after = lax.dynamic_update_slice_in_dim(
+                after, oldest, (b_next + dev_j) % small * reply, axis=0
+            )
+    return after
 
 
 def einsum_mixed(form, left, right):
@@ -239,7 +266,7 @@
         lax.all_gather(ada_weight[layer_idx], "fsdp", axis=0, tiled=True),
         lax.all_gather(ada_bias[layer_idx], "fsdp", axis=0, tiled=True),
         lax.all_gather(qkv_weight[layer_idx], "fsdp", axis=0, tiled=True),
-        lax.all_gather(proj_weight[layer_idx], "fsdp", axis=0, tiled=True),
+        arrange_regions(proj_weight[layer_idx]),
         lax.all_gather(proj_bias[layer_idx], "fsdp", axis=0, tiled=True),
         lax.all_gather(up_weight[layer_idx], "fsdp", axis=0, tiled=True),
         lax.all_gather(up_bias[layer_idx], "fsdp", axis=0, tiled=True),

time: 738 us -> 733 us (level)
  waiting for transfers between devices: 379 us -> 355 us
    reduce_scatter x2, waiting for transfers between devices: 16.1 us -> 0.13 us  [reduce_layer(): lax.psum_scatter(grads[2], 'fsdp', scatter_dimension=0, tiled=True)]
    psum x1, waiting for transfers between devices: 129 us -> 117 us  [reduce_layer(): lax.psum((shards[0], shards[1], shards[2], shards[3], shards[4], shards[5...]
    dot_general x8 -> x12, matrix products: 28.3 us -> 37.6 us  [matmul_last(): jnp.dot(flat, right, preferred_element_type=jnp.float32)]
    unnamed x273 -> x295, local copies, waits for them, and re-layouts: 18.8 us -> 21.2 us
  transfers between devices with their start and end apart: 17 -> 23, of which waited for: 9 -> 12; matrix products, arithmetic and copies ran while one was open for 20% -> 23% of each run, Pallas kernels for 0% -> 0%
where the time goes in v1:
time: 733 us; the launch traced here: 726 us
  waiting for transfers between devices  355 us (48%)
  matrix products  162 us (22%)
  blocking collectives  112 us (15%)
  local copies, waits for them, and re-layouts  38.7 us (5%)
  other arithmetic  33.3 us (5%)
  between operations  19.5 us (3%)
    psum x1, waiting for transfers between devices, reduce_layer(): lax.psum((shards[0], shards[1], shards[2], shards[3], shards[4], shards[5...  117 us
    reduce_scatter x2, waiting for transfers between devices, reduce_layer(): lax.psum_scatter(grads[0], 'fsdp', scatter_dimension=0, tiled=True)  85.6 us
    reduce_scatter x2, waiting for transfers between devices, reduce_layer(): lax.psum_scatter(grads[7], 'fsdp', scatter_dimension=0, tiled=True)  70.8 us
    reduce_scatter x2, waiting for transfers between devices, reduce_layer(): lax.psum_scatter(grads[5], 'fsdp', scatter_dimension=0, tiled=True)  70.5 us
    dot_general x12, matrix products, einsum_mixed(): return jnp.einsum(form, left, right, preferred_element_type=jnp.float32)  57.9 us
    psum x1, blocking collectives, reduce_layer(): lax.psum((shards[0], shards[1], shards[2], shards[3], shards[4], shards[5...  40 us
    dot_general x12, matrix products, matmul_last(): jnp.dot(flat, right, preferred_element_type=jnp.float32)  37.6 us
    dot_general x8, matrix products, outer_total(): jnp.dot(left.reshape(-1, left.shape[-1]).T, right.reshape(-1, right.shape...  31 us
  transfers between devices with their start and end apart: 23, of which 12 were waited for; matrix products, arithmetic and copies ran while one was open for 23% of the time, Pallas kernels for 0%

profile of v1, /device:TPU:0, one launch (start us, length us, event | category | flops | bytes accessed | tf_op | source)
XLA Modules:
  0.0 726.4 jit_solution(9228827964230624960)
XLA Ops:
  19.8 5.6 all-gather.13
  26.0 5.7 all-gather.5
  33.6 12.2 %all-reduce.17 = (bf16[2304]{0:T(1024)(128)(2,1)S(1)}, bf16[384]{0:T(512)(128)(2,1)S(1)}, bf16[384]{0:T(512)(128)(2,1)S(1)}, bf16[2304]{0:T(1024)(128)(2,1)S(1)}...) all-reduce(bf16[2304]{0:T(1024)(128)(2,1)S(1)} %dynamic-update-slice, ...), channel_id=3, replica_groups=mesh['dp'=8,'fsdp'=4] {'fsdp'}, use_global_device_ids=true, to_apply=%add | all-reduce | flops 6144 | bytes 24576
  46.9 8.1 %all-gather.16 = bf16[1,384,384]{2,1,0:T(8,128)(2,1)} all-gather(bf16[1,96,384]{2,1,0:T(8,128)(2,1)S(1)} %get-tuple-element.83), channel_id=18, replica_groups=mesh['dp'=8,'fsdp'=4] {'fsdp'}, dimensions={1}, use_global_device_ids=true | all-gather | bytes 368640 | tf_op jit(solution)/shard_map/all_gather | solution.py:294
  55.1 9.7 %all-gather.10 = bf16[1,384,1152]{2,1,0:T(8,128)(2,1)} all-gather(bf16[1,96,1152]{2,1,0:T(8,128)(2,1)S(1)} %get-tuple-element.81), channel_id=12, replica_groups=mesh['dp'=8,'fsdp'=4] {'fsdp'}, dimensions={1}, use_global_device_ids=true | all-gather | bytes 1105920 | tf_op jit(solution)/shard_map/all_gather | solution.py:268
  64.7 12.8 %all-gather.2 = bf16[1,384,1152]{2,1,0:T(8,128)(2,1)S(1)} all-gather(bf16[1,96,1152]{2,1,0:T(8,128)(2,1)S(1)} %get-tuple-element.82), channel_id=4, replica_groups=mesh['dp'=8,'fsdp'=4] {'fsdp'}, dimensions={1}, use_global_device_ids=true | all-gather | bytes 1105920 | tf_op jit(solution)/shard_map/all_gather | solution.py:268
  77.6 6.5 all-gather.17
  106.8 5.2 fusion.202
  139.3 7.2 fusion.207
  161.0 9.1 %fusion.90 = bf16[3,256,1,6,64]{1,4,3,0,2:T(8,128)(2,1)} fusion(f32[3,6,256,256]{2,3,1,0:T(8,128)} %fusion.157, bf16[3,256,3,6,64]{1,4,3,2,0:T(8,128)(2,1)} %bitcast.265, f32[3,6,256,256]{2,3,1,0:T(8,128)} %copy-done.27, f32[3,6,256]{2,1,0:T(8,128)S(1)} %copy-done.92), kind=kOutput, calls=%fused_computation.109 | convolution fusion | flops 159552256 | bytes 20103168 | tf_op jit(solution)/shard_map/shqk,skhd->sqhd/dot_general | solution.py:41
  170.1 9.1 %fusion.87 = bf16[3,256,1,6,64]{1,4,3,0,2:T(8,128)(2,1)} fusion(f32[3,6,256,256]{2,3,1,0:T(8,128)} %fusion.157, bf16[3,256,3,6,64]{1,4,3,2,0:T(8,128)(2,1)} %bitcast.266, f32[3,6,256,256]{2,3,1,0:T(8,128)} %copy-done.27, f32[3,6,256]{2,1,0:T(8,128)S(1)} %copy-done.92), kind=kOutput, calls=%fused_computation.108 | convolution fusion | flops 159552256 | bytes 20103168 | tf_op jit(solution)/shard_map/shqk,sqhd->skhd/dot_general | solution.py:41
  220.5 9.1 %fusion.96 = bf16[3,256,1,6,64]{1,4,3,0,2:T(8,128)(2,1)} fusion(f32[3,6,256,256]{2,3,1,0:T(8,128)} %fusion.155, bf16[3,256,3,6,64]{1,4,3,2,0:T(8,128)(2,1)} %bitcast.260, f32[3,6,256,256]{2,3,1,0:T(8,128)} %copy-done.26, f32[3,6,256]{2,1,0:T(8,128)} %copy-done.90), kind=kOutput, calls=%fused_computation.111 | convolution fusion | flops 159552256 | bytes 20103168 | tf_op jit(solution)/shard_map/shqk,skhd->sqhd/dot_general | solution.py:41
  229.6 9.0 %fusion.93 = bf16[3,256,1,6,64]{1,4,3,0,2:T(8,128)(2,1)} fusion(f32[3,6,256,256]{2,3,1,0:T(8,128)} %fusion.155, bf16[3,256,3,6,64]{1,4,3,2,0:T(8,128)(2,1)} %bitcast.261, f32[3,6,256,256]{2,3,1,0:T(8,128)} %copy-done.26, f32[3,6,256]{2,1,0:T(8,128)} %copy-done.90), kind=kOutput, calls=%fused_computation.110 | convolution fusion | flops 159552256 | bytes 20103168 | tf_op jit(solution)/shard_map/shqk,sqhd->skhd/dot_general | solution.py:41
  247.3 6.5 convolution_bitcast_fusion
  260.0 6.3 convolution_bitcast_fusion.1
  295.2 35.4 %reduce-scatter.29.cloned.1.call-done = f32[384,384]{1,0:T(8,128)} async-done(((f32[1536,384]{1,0:T(8,128)}), f32[384,384]{1,0:T(8,128)}) %reduce-scatter.29.cloned.1.call-update) | async-done | bytes 589840 | tf_op jit(solution)/shard_map/reduce_scatter | solution.py:312
  330.6 35.2 %reduce-scatter.25.cloned.1.call-done = f32[96,1536]{1,0:T(8,128)} async-done(((f32[384,1536]{1,0:T(8,128)}), f32[96,1536]{1,0:T(8,128)}) %reduce-scatter.25.cloned.1.call-update) | async-done | bytes 589840 | tf_op jit(solution)/shard_map/reduce_scatter | solution.py:310
  365.8 35.4 %reduce-scatter.27.cloned.1.call-done = f32[384,384]{1,0:T(8,128)} async-done(((f32[1536,384]{1,0:T(8,128)}), f32[384,384]{1,0:T(8,128)}) %reduce-scatter.27.cloned.1.call-update) | async-done | bytes 589840 | tf_op jit(solution)/shard_map/reduce_scatter | solution.py:312
  401.2 35.2 %reduce-scatter.23.cloned.1.call-done = f32[96,1536]{1,0:T(8,128)} async-done(((f32[384,1536]{1,0:T(8,128)}), f32[96,1536]{1,0:T(8,128)}) %reduce-scatter.23.cloned.1.call-update) | async-done | bytes 589840 | tf_op jit(solution)/shard_map/reduce_scatter | solution.py:310
  436.4 42.8 %reduce-scatter.13.cloned.1.call-done = f32[96,2304]{1,0:T(8,128)} async-done(((f32[384,2304]{1,0:T(8,128)}), f32[96,2304]{1,0:T(8,128)}) %reduce-scatter.13.cloned.1.call-update) | async-done | bytes 884752 | tf_op jit(solution)/shard_map/reduce_scatter | solution.py:305
  479.2 42.8 %reduce-scatter.11.cloned.1.call-done = f32[96,2304]{1,0:T(8,128)} async-done(((f32[384,2304]{1,0:T(8,128)}), f32[96,2304]{1,0:T(8,128)}) %reduce-scatter.11.cloned.1.call-update) | async-done | bytes 884752 | tf_op jit(solution)/shard_map/reduce_scatter | solution.py:305
  530.6 11.0 %all-reduce.16 = (f32[2304]{0:T(1024)S(1)}, f32[2304]{0:T(1024)S(1)}, f32[384]{0:T(512)S(1)}, f32[384]{0:T(512)S(1)}, f32[1536]{0:T(1024)S(1)}, /*index=5*/f32[1536]{0:T(1024)S(1)}, f32[384]{0:T(512)S(1)}, f32[384]{0:T(512)S(1)}) all-reduce(f32[2304]{0:T(1024)S(1)} %reduce_sum.457, ...), channel_id=23, replica_groups=mesh['dp'=8,'fsdp'=4] {'fsdp'}, use_global_device_ids=true, to_apply=%region_46.47.clone | all-reduce | flops 9216 | bytes 73728
  542.2 40.0 %all-reduce.14 = (f32[1,576]{1,0:T(1,128)S(1)}, f32[1,576]{1,0:T(1,128)S(1)}, f32[1,96]{1,0:T(1,128)S(1)}, f32[1,96]{1,0:T(1,128)S(1)}, f32[1,384]{1,0:T(1,128)S...) all-reduce(f32[1,576]{1,0:T(1,128)S(1)} %stack.125, ...), channel_id=1, replica_groups=mesh['dp'=8,'fsdp'=4] {'dp'}, use_global_device_ids=true, to_apply=%region_47.48 | all-reduce | flops 2304 | bytes 18432 | tf_op jit(solution)/shard_map/psum | solution.py:315
  595.6 117.3 %all-reduce.20.cloned.1.call-done = (f32[1,96,2304]{2,1,0:T(8,128)}, f32[1,96,2304]{2,1,0:T(8,128)}, f32[1,96,1152]{2,1,0:T(8,128)}, f32[1,96,1152]{2,1,0:T(8,12...) async-done(((f32[1,96,2304]{2,1,0:T(8,128)}, ...) | async-done | bytes 5308432 | tf_op jit(solution)/shard_map/psum | solution.py:315
  (482 shorter events, 189.8 us)
Async XLA Ops:
  7.2 80.7 %all-gather.25.cloned.1.call-start = ((), (), s32[]{:S(2)}) async-start(), calls=%async_computation.20 | async-start | bytes 2211840 | tf_op jit(solution)/shard_map/all_gather | solution.py:266
  9.5 80.9 %all-gather.31.cloned.1.call-start = ((), (), s32[]{:S(2)}) async-start(), calls=%async_computation.23 | async-start | bytes 2211840 | tf_op jit(solution)/shard_map/all_gather | solution.py:266
  10.2 96.6 %all-gather.27.cloned.1.call-start = ((), (), s32[]{:S(2)}) async-start(), calls=%async_computation.21 | async-start | bytes 1474560 | tf_op jit(solution)/shard_map/all_gather | solution.py:271
  11.2 95.6 %all-gather.29.cloned.1.call-start = ((), (), s32[]{:S(2)}) async-start(), calls=%async_computation.22 | async-start | bytes 1474560 | tf_op jit(solution)/shard_map/all_gather | solution.py:273
  12.1 119.0 %all-gather.33.cloned.1.call-start = ((), (), s32[]{:S(2)}) async-start(), calls=%async_computation.24 | async-start | bytes 1474560 | tf_op jit(solution)/shard_map/all_gather | solution.py:271
  12.7 126.6 %all-gather.35.cloned.1.call-start = ((), (), s32[]{:S(2)}) async-start(), calls=%async_computation.25 | async-start | bytes 1474560 | tf_op jit(solution)/shard_map/all_gather | solution.py:273
  13.4 70.7 %collective-permute-start = (bf16[96,384]{1,0:T(8,128)(2,1)S(1)}, bf16[96,384]{1,0:T(8,128)(2,1)S(1)}, u32[]{:S(2)}, u32[]{:S(2)}) collective-permute-start(bf16[96,384]{1,0:T(8,128)(2,1)S(1)} %get-tuple-element.84), channel_id=1, source_target_pairs={{0,1},{1,2},{2,3},{3,0},{4,5},{5,6},{6,7},{7,4},{8,9},{9,10},{10,1... | collective-permute-start | bytes 221192 | tf_op jit(solution)/shard_map/ppermute | solution.py:28
  13.9 70.5 %collective-permute-start.1 = (bf16[96,384]{1,0:T(8,128)(2,1)S(1)}, bf16[96,384]{1,0:T(8,128)(2,1)S(1)}, u32[]{:S(2)}, u32[]{:S(2)}) collective-permute-start(bf16[96,384]{1,0:T(8,128)(2,1)S(1)} %get-tuple-element.84), channel_id=1, source_target_pairs={{0,3},{1,0},{2,1},{3,2},{4,7},{5,4},{6,5},{7,6},{8,11},{9,8},{10,9... | collective-permute-start | bytes 221192 | tf_op jit(solution)/shard_map/ppermute | solution.py:33
  15.9 279.1 %reduce-scatter.21.cloned.1.call-start = ((), (), s32[]{:S(2)}) async-start(), calls=%async_computation.15 | async-start | bytes 737280 | tf_op jit(solution)/shard_map/reduce_scatter | solution.py:308
  19.4 73.6 %copy-start.75 = (f32[3,256]{1,0:T(4,128)}, f32[3,256]{1,0:T(4,128)S(1)}, u32[]{:S(2)}) copy-start(f32[3,256]{1,0:T(4,128)S(1)} %broadcast_multiply_fusion.13) | copy-start | bytes 9220
  84.1 3.8 collective-permute-start.2
  184.9 110.1 %reduce-scatter.19.cloned.1.call-start = ((), (), s32[]{:S(2)}) async-start(), calls=%async_computation.14 | async-start | bytes 737280 | tf_op jit(solution)/shard_map/reduce_scatter | solution.py:308
  206.9 88.2 %reduce-scatter.17.cloned.1.call-start = ((), (), s32[]{:S(2)}) async-start(), calls=%async_computation.13 | async-start | bytes 2211840 | tf_op jit(solution)/shard_map/reduce_scatter | solution.py:307
  211.3 83.9 %reduce-scatter.15.cloned.1.call-start = ((), (), s32[]{:S(2)}) async-start(), calls=%async_computation.12 | async-start | bytes 2211840 | tf_op jit(solution)/shard_map/reduce_scatter | solution.py:307
  246.6 84.0 %reduce-scatter.29.cloned.1.call-start = ((), (), s32[]{:S(2)}) async-start(), calls=%async_computation.19 | async-start | bytes 2949120 | tf_op jit(solution)/shard_map/reduce_scatter | solution.py:312
  253.8 112.0 %reduce-scatter.25.cloned.1.call-start = ((), (), s32[]{:S(2)}) async-start(), calls=%async_computation.17 | async-start | bytes 2949120 | tf_op jit(solution)/shard_map/reduce_scatter | solution.py:310
  258.8 142.4 %reduce-scatter.27.cloned.1.call-start = ((), (), s32[]{:S(2)}) async-start(), calls=%async_computation.18 | async-start | bytes 2949120 | tf_op jit(solution)/shard_map/reduce_scatter | solution.py:312
  266.4 170.0 %reduce-scatter.23.cloned.1.call-start = ((), (), s32[]{:S(2)}) async-start(), calls=%async_computation.16 | async-start | bytes 2949120 | tf_op jit(solution)/shard_map/reduce_scatter | solution.py:310
  271.4 207.8 %reduce-scatter.13.cloned.1.call-start = ((), (), s32[]{:S(2)}) async-start(), calls=%async_computation.11 | async-start | bytes 4423680 | tf_op jit(solution)/shard_map/reduce_scatter | solution.py:305
  282.9 239.1 %reduce-scatter.11.cloned.1.call-start = ((), (), s32[]{:S(2)}) async-start(), calls=%async_computation.10 | async-start | bytes 4423680 | tf_op jit(solution)/shard_map/reduce_scatter | solution.py:305
  295.0 418.0 %all-reduce.20.cloned.1.call-start = ((), (), s32[]{:S(2)}) async-start(), calls=%async_computation.26 | async-start | bytes 10616832 | tf_op jit(solution)/shard_map/psum | solution.py:315
  522.2 4.3 collective-permute-start.3
  522.2 5.1 collective-permute-start.4
  526.5 4.0 collective-permute-start.5
  (131 other events, 926.0 us)
Sparse Core Ops, SparseCore 0:
  10.1 23.5 all-gather.24
  35.9 22.2 all-gather.30
  60.4 20.4 all-gather.26
  82.9 18.0 all-gather.28
  102.4 17.4 all-gather.32
  121.9 17.4 all-gather.34
  185.1 22.0 reduce-scatter.20
  209.7 22.0 reduce-scatter.18
  234.3 29.1 reduce-scatter.16
  266.0 29.1 reduce-scatter.14
  297.7 32.8 reduce-scatter.28
  333.0 32.8 reduce-scatter.24
  368.4 32.8 reduce-scatter.26
  403.6 32.8 reduce-scatter.22
  438.9 40.3 reduce-scatter.12
  481.7 40.3 reduce-scatter.10
  526.7 186.2 all-reduce.19
